TPU v7x, 32 devices: a whole 2x2x4 slice. The times are simulated.
32 devices in a mesh: rows: 8 (over z, x), tm: 4 (over y, core).
Axes of the slice: x: 2, y: 2, z: 4, core: 2. Of those that a mesh axis runs over, the one named last changes fastest.
Arguments:
- snapshots: bfloat16 [262144, 512], P('rows', 'tm'), may hold values from -6 to 6
- modes: bfloat16 [262144, 256], P('rows'), may hold values from -0.01171875 to 0.01171875
- eig_vectors: float32 [3, 256], replicated, may hold values from -0.375 to 0.375
- eig_values: float32 [3], replicated, may hold values from -1 to 1
Outputs:
- operator: float32 [256, 256], replicated
- eig_residual: float32 [3, 256], replicated
- residual_norm: float32 [3], replicated
All inputs are finite; a program needn't handle non-finite values.
Results may differ from a plain program's by a relative error of at most 0.0003.
Values may be sent and summed in bfloat16 or wider, within the bound.
A program may use at most 128 MiB of HBM per device.

v0:
```python
import jax
import jax.numpy as jnp
from jax import lax
from jax.sharding import PartitionSpec as P


def pair_terms(coords, after, keep):
    lead = coords * keep
    trail = jnp.concatenate([coords[:, 1:], after], axis=1)
    cross_part = jnp.dot(
        trail, lead.T, precision=lax.Precision.HIGHEST, preferred_element_type=jnp.float32
    )
    gram_part = jnp.dot(
        lead, lead.T, precision=lax.Precision.HIGHEST, preferred_element_type=jnp.float32
    )
    return (cross_part, gram_part)


def body(snapshots, modes, eig_vectors, eig_values):
    block_cols = snapshots.shape[1]
    width = modes.shape[1]
    time_count = lax.axis_size("tm")
    total_cols = block_cols * time_count
    partial_value = jnp.einsum("mr,mt->rt", modes, snapshots, preferred_element_type=jnp.float32)
    coords = lax.psum(partial_value, "rows")
    series = lax.all_gather(coords, "tm", axis=1, tiled=True)
    every = lax.broadcasted_iota(jnp.int32, (1, total_cols), 1)
    whole_keep = (every < total_cols - 1).astype(jnp.float32)
    zero_col = jnp.zeros((width, 1), jnp.float32)
    cross, gram = pair_terms(series, zero_col, whole_keep)
    scale = jnp.float32(total_cols - 1)
    cross = cross / scale
    gram = gram / scale + jnp.eye(width, dtype=jnp.float32)
    factor = jnp.linalg.cholesky(gram)
    operator = jax.scipy.linalg.cho_solve((factor, True), cross.T).T
    eig_residual = (
        jnp.dot(
            eig_vectors,
            operator.T,
            precision=lax.Precision.HIGHEST,
            preferred_element_type=jnp.float32,
        )
        - eig_values[:, None] * eig_vectors
    )
    residual_norm = jnp.sqrt(jnp.sum(eig_residual * eig_residual, axis=1) + 1e-06)
    return (operator, eig_residual, residual_norm)


def solution(mesh):
    return jax.shard_map(
        body,
        mesh=mesh,
        in_specs=(P("rows", "tm"), P("rows", None), P(), P()),
        out_specs=(P(), P(), P()),
        check_vma=False,
    )
```

profile of v0, /device:TPU:0, one launch (start us, length us, event | category | flops | bytes accessed | tf_op | source)
XLA Modules:
  0.0 174.0 jit_solution(5392952128399339872)
XLA Ops:
  7.2 0.0 copy-start
  7.2 0.0 copy-start.1
  7.2 0.0 all-reduce.4.cloned.1.call-start
  7.2 13.4 %fusion.23 = f32[256,128]{1,0:T(8,128)} fusion(bf16[32768,256]{1,0:T(8,128)(2,1)} %param.5, bf16[32768,128]{1,0:T(8,128)(2,1)} %param.4), kind=kOutput, calls=%fused_computation.53 | convolution fusion | flops 2147483648 | bytes 25296896 | tf_op jit(solution)/shard_map/mr,mt->rt/dot_general | solution.py:24
  20.6 0.0 all-reduce.4.cloned.1.call-update
  20.7 73.3 %all-reduce.4.cloned.1.call-done = f32[256,128]{1,0:T(8,128)} async-done(((f32[256,128]{1,0:T(8,128)}), f32[256,128]{1,0:T(8,128)}) %all-reduce.4.cloned.1.call-update) | async-done | bytes 131088 | tf_op jit(solution)/shard_map/psum | solution.py:25
  94.0 7.5 %all_gather.3 = f32[256,512]{1,0:T(8,128)S(1)} all-gather(f32[256,128]{1,0:T(8,128)} %all-reduce.4.cloned.1.call-done), channel_id=1, replica_groups=mesh['rows'=8,'tm'=4] {'tm'}, dimensions={1}, use_global_device_ids=true | all-gather | bytes 655360 | tf_op jit(solution)/shard_map/all_gather | solution.py:26
  101.5 0.2 slice.77
  101.7 0.6 convert_add_fusion
  102.4 0.6 convolution_multiply_fusion
  103.0 0.1 copy.8
  103.2 11.7 %cholesky.50 = f32[128,128]{1,0:T(8,128)S(1)} custom-call(f32[128,128]{1,0:T(8,128)S(1)} %cholesky.118), custom_call_target="Cholesky" | custom-call | tf_op jit(solution)/shard_map/jit(cholesky)/cholesky | solution.py:34
  115.0 9.8 %custom-call.18 = f32[1,128,128]{1,2,0:T(8,128)S(1)} custom-call(f32[1,128,128]{2,1,0:T(8,128)S(1)} %get-tuple-element.27), custom_call_target="InvertDiagBlocksLowerTriangular" | custom-call | tf_op jit(solution)/shard_map/jit(cholesky)/cholesky | solution.py:34
  124.8 0.2 constant_dynamic-update-slice_fusion.1
  125.0 0.3 convolution_subtract_fusion.2
  125.3 11.7 %cholesky.105 = f32[128,128]{1,0:T(8,128)S(1)} custom-call(f32[128,128]{1,0:T(8,128)S(1)} %convolution_subtract_fusion.2), custom_call_target="Cholesky" | custom-call | tf_op jit(solution)/shard_map/jit(cholesky)/cholesky | solution.py:34
  137.0 0.6 compare_reduce_fusion
  139.0 0.1 triangular_solve.72
  139.1 4.2 %while.1 = (s32[]{:T(128)}, f32[256,256]{1,0:T(8,128)S(1)}, s32[2,2]{1,0:T(2,128)S(1)}, f32[2,128,128]{2,1,0:T(8,128)S(1)}, s32[]{:T(128)}) while((s32[]{:T(128)}, f32[256,256]{1,0:T(8,128)S(1)}, s32[2,2]{1,0:T(2,128)S(1)}, f32[2,128,128]{2,1,0:T(8,128)S(1)}, s32[]{:T(128)}) %tuple.30), condition=%wide.while_cond, body=%wide.while_body.sunk | while | flops 2 | bytes 131189 | solution.py:35
  139.3 0.6 fusion.35
  139.9 1.4 bitcast_dynamic-update-slice_fusion.2
  141.3 0.6 fusion.35
  141.9 1.4 bitcast_dynamic-update-slice_fusion.2
  143.3 19.7 %custom-call.19 = f32[2,128,128]{1,2,0:T(8,128)S(1)} custom-call(f32[2,128,128]{2,1,0:T(8,128)S(1)} %get-tuple-element.10), custom_call_target="InvertDiagBlocksLowerTriangular" | custom-call | tf_op jit(solution)/shard_map/jit(_cho_solve)/triangular_solve | solution.py:35
  162.9 0.3 fusion.9
  163.3 0.4 convolution_subtract_fusion.1
  163.7 0.3 fusion.16
  164.0 0.3 fusion.15
  164.2 0.3 convolution_subtract_fusion
  164.6 0.3 fusion.14
  164.9 0.8 copy.10
  165.7 0.0 copy-done
  165.7 0.0 copy-done.1
  165.7 1.0 multiply_reduce_fusion
  166.7 0.5 add_sqrt_fusion
  (12 shorter events, 0.2 us)
Async XLA Ops:
  7.2 158.5 %copy-start = (f32[3,256]{1,0:T(4,128)S(1)}, f32[3,256]{1,0:T(4,128)}, u32[]{:S(2)}) copy-start(f32[3,256]{1,0:T(4,128)} %param.6) | copy-start | bytes 9220
  7.2 158.5 %copy-start.1 = (f32[3]{0:T(128)S(1)}, f32[3]{0:T(128)}, u32[]{:S(2)}) copy-start(f32[3]{0:T(128)} %param.7) | copy-start | bytes 40
  7.2 86.8 %all-reduce.4.cloned.1.call-start = ((), (), s32[]{:S(2)}) async-start(), calls=%async_computation | async-start | bytes 262144 | tf_op jit(solution)/shard_map/psum | solution.py:25
Sparse Core Ops, SparseCore 0:
  20.8 73.1 all-reduce.3
where the time goes:
time: 174 us
  waiting for transfers between devices  73.3 us (42%)
  other arithmetic  54.2 us (31%)
  matrix products  17.9 us (10%)
  between operations  15.5 us (9%)
  blocking collectives  7.53 us (4%)
  local copies, waits for them, and re-layouts  5.22 us (3%)
    psum x1, waiting for transfers between devices, body(): coords = lax.psum(partial_value, 'rows')  73.3 us
    another operation x6, other arithmetic, body(): factor = jnp.linalg.cholesky(gram)  33.9 us
    another operation x3, other arithmetic, body(): operator = jax.scipy.linalg.cho_solve((factor, True), cross.T).T  19.7 us
    dot_general x1, matrix products, body(): jnp.einsum('mr,mt->rt', modes, snapshots, preferred_element_type=jnp.floa...  13.4 us
    all_gather x1, blocking collectives, body(): series = lax.all_gather(coords, 'tm', axis=1, tiled=True)  7.53 us
    another operation x6, local copies, waits for them, and re-layouts  3.95 us
  transfers between devices with their start and end apart: 1, of which 1 were waited for; matrix products, arithmetic and copies ran while one was open for 0% of the time, Pallas kernels for 0%

commit v1 on v0

--- a/solution.py
+++ b/solution.py
@@ -2,6 +2,11 @@
 import jax.numpy as jnp
 from jax import lax
 from jax.sharding import PartitionSpec as P
+
+
+def gather_and_add(block, axis):
+    parts = lax.all_gather(block, axis)
+    return jnp.sum(parts, axis=0)
 
 
 def pair_terms(coords, after, keep):
@@ -22,7 +27,7 @@
     time_count = lax.axis_size("tm")
     total_cols = block_cols * time_count
     partial_value = jnp.einsum("mr,mt->rt", modes, snapshots, preferred_element_type=jnp.float32)
-    coords = lax.psum(partial_value, "rows")
+    coords = gather_and_add(partial_value, "rows")
     series = lax.all_gather(coords, "tm", axis=1, tiled=True)
     every = lax.broadcasted_iota(jnp.int32, (1, total_cols), 1)
     whole_keep = (every < total_cols - 1).astype(jnp.float32)

time: 174 us -> 145 us (0.83)
  waiting for transfers between devices: 73.3 us -> 43.1 us
    psum x1 -> x0, waiting for transfers between devices: 73.3 us -> none  [body(): coords = lax.psum(partial_value, 'rows')]
    all_gather x0 -> x1, waiting for transfers between devices: none -> 43.1 us  [gather_and_add(): parts = lax.all_gather(block, axis)]
where the time goes in v1:
time: 145 us
  other arithmetic  55.5 us (38%)
  waiting for transfers between devices  43.1 us (30%)
  matrix products  17.9 us (12%)
  between operations  15.5 us (11%)
  blocking collectives  7.34 us (5%)
  local copies, waits for them, and re-layouts  5.22 us (4%)
    all_gather x1, waiting for transfers between devices, gather_and_add(): parts = lax.all_gather(block, axis)  43.1 us
    another operation x6, other arithmetic, body(): factor = jnp.linalg.cholesky(gram)  33.9 us
    another operation x3, other arithmetic, body(): operator = jax.scipy.linalg.cho_solve((factor, True), cross.T).T  19.7 us
    dot_general x1, matrix products, body(): jnp.einsum('mr,mt->rt', modes, snapshots, preferred_element_type=jnp.floa...  13.4 us
    all_gather x1, blocking collectives, body(): series = lax.all_gather(coords, 'tm', axis=1, tiled=True)  7.34 us
    another operation x6, local copies, waits for them, and re-layouts  3.95 us
  transfers between devices with their start and end apart: 1, of which 1 were waited for; matrix products, arithmetic and copies ran while one was open for 0% of the time, Pallas kernels for 0%

profile of v1, /device:TPU:0, one launch (start us, length us, event | category | flops | bytes accessed | tf_op | source)
XLA Modules:
  0.0 144.9 jit_solution(623486617830757040)
XLA Ops:
  7.2 0.0 copy-start
  7.2 0.0 copy-start.1
  7.2 0.0 all-gather.3.cloned.1.call-start
  7.2 13.4 %fusion.23 = f32[256,128]{1,0:T(8,128)} fusion(bf16[32768,256]{1,0:T(8,128)(2,1)} %param.5, bf16[32768,128]{1,0:T(8,128)(2,1)} %param.4), kind=kOutput, calls=%fused_computation.53 | convolution fusion | flops 2147483648 | bytes 25296896 | tf_op jit(solution)/shard_map/mr,mt->rt/dot_general | solution.py:29
  20.6 0.0 all-gather.3.cloned.1.call-update
  20.7 43.1 %all-gather.3.cloned.1.call-done = f32[2048,128]{1,0:T(8,128)} async-done(((f32[256,128]{1,0:T(8,128)}), f32[2048,128]{1,0:T(8,128)}) %all-gather.3.cloned.1.call-update) | async-done | bytes 1048592 | tf_op jit(solution)/shard_map/all_gather | solution.py:8
  63.8 1.3 reduce_sum.18
  65.1 7.3 %all_gather.11 = f32[256,512]{1,0:T(8,128)S(1)} all-gather(f32[256,128]{1,0:T(8,128)S(1)} %reduce_sum.18), channel_id=1, replica_groups=mesh['rows'=8,'tm'=4] {'tm'}, dimensions={1}, use_global_device_ids=true | all-gather | bytes 655360 | tf_op jit(solution)/shard_map/all_gather | solution.py:31
  72.4 0.2 slice.77
  72.6 0.6 convert_add_fusion
  73.3 0.1 copy.8
  73.5 11.7 %cholesky.50 = f32[128,128]{1,0:T(8,128)S(1)} custom-call(f32[128,128]{1,0:T(8,128)S(1)} %cholesky.118), custom_call_target="Cholesky" | custom-call | tf_op jit(solution)/shard_map/jit(cholesky)/cholesky | solution.py:39
  85.2 0.6 convolution_multiply_fusion
  85.9 9.8 %custom-call.18 = f32[1,128,128]{1,2,0:T(8,128)S(1)} custom-call(f32[1,128,128]{2,1,0:T(8,128)S(1)} %get-tuple-element.27), custom_call_target="InvertDiagBlocksLowerTriangular" | custom-call | tf_op jit(solution)/shard_map/jit(cholesky)/cholesky | solution.py:39
  95.7 0.2 constant_dynamic-update-slice_fusion.1
  95.9 0.3 convolution_subtract_fusion.2
  96.2 11.7 %cholesky.105 = f32[128,128]{1,0:T(8,128)S(1)} custom-call(f32[128,128]{1,0:T(8,128)S(1)} %convolution_subtract_fusion.2), custom_call_target="Cholesky" | custom-call | tf_op jit(solution)/shard_map/jit(cholesky)/cholesky | solution.py:39
  107.9 0.6 compare_reduce_fusion
  109.9 0.1 triangular_solve.72
  110.0 4.2 %while.1 = (s32[]{:T(128)}, f32[256,256]{1,0:T(8,128)S(1)}, s32[2,2]{1,0:T(2,128)S(1)}, f32[2,128,128]{2,1,0:T(8,128)S(1)}, s32[]{:T(128)}) while((s32[]{:T(128)}, f32[256,256]{1,0:T(8,128)S(1)}, s32[2,2]{1,0:T(2,128)S(1)}, f32[2,128,128]{2,1,0:T(8,128)S(1)}, s32[]{:T(128)}) %tuple.30), condition=%wide.while_cond, body=%wide.while_body.sunk | while | flops 2 | bytes 131189 | solution.py:40
  110.2 0.6 fusion.35
  110.7 1.4 bitcast_dynamic-update-slice_fusion.2
  112.2 0.6 fusion.35
  112.7 1.4 bitcast_dynamic-update-slice_fusion.2
  114.1 19.7 %custom-call.19 = f32[2,128,128]{1,2,0:T(8,128)S(1)} custom-call(f32[2,128,128]{2,1,0:T(8,128)S(1)} %get-tuple-element.10), custom_call_target="InvertDiagBlocksLowerTriangular" | custom-call | tf_op jit(solution)/shard_map/jit(_cho_solve)/triangular_solve | solution.py:40
  133.8 0.3 fusion.9
  134.1 0.4 convolution_subtract_fusion.1
  134.5 0.3 fusion.16
  134.9 0.3 fusion.15
  135.1 0.3 convolution_subtract_fusion
  135.4 0.3 fusion.14
  135.7 0.8 copy.10
  136.6 0.0 copy-done
  136.6 0.0 copy-done.1
  136.6 1.0 multiply_reduce_fusion
  137.5 0.5 add_sqrt_fusion
  (12 shorter events, 0.2 us)
Async XLA Ops:
  7.2 129.4 %copy-start = (f32[3,256]{1,0:T(4,128)S(1)}, f32[3,256]{1,0:T(4,128)}, u32[]{:S(2)}) copy-start(f32[3,256]{1,0:T(4,128)} %param.6) | copy-start | bytes 9220
  7.2 129.4 %copy-start.1 = (f32[3]{0:T(128)S(1)}, f32[3]{0:T(128)}, u32[]{:S(2)}) copy-start(f32[3]{0:T(128)} %param.7) | copy-start | bytes 40
  7.2 56.6 %all-gather.3.cloned.1.call-start = ((), (), s32[]{:S(2)}) async-start(), calls=%async_computation | async-start | bytes 1179648 | tf_op jit(solution)/shard_map/all_gather | solution.py:8
Sparse Core Ops, SparseCore 0:
  20.8 42.9 all-gather.2
